TPU v7x, 256 devices: a whole 4x4x8 slice. The times are simulated.
256 devices in a mesh: tile: 64 (over x, z, core), rep: 4 (over y).
Axes of the slice: x: 4, y: 4, z: 8, core: 2. Of those that a mesh axis runs over, the one named last changes fastest.
Arguments:
- stamps: bfloat16 [625, 262144], P(None, ('tile', 'rep')), may hold values from -6 to 6
- spread_coefficients: bfloat16 [4, 10, 262144], P(None, None, ('tile', 'rep')), may hold values from -2.5 to 2.5
- stamp_ivar: bfloat16 [262144], P(('tile', 'rep')), may hold values from 0.5 to 4
- stamp_ccd: int32 [262144], P(('tile', 'rep')), may hold values from 0 to 3
- psf_bases: bfloat16 [1024, 10, 625], P(('tile', 'rep')), may hold values from -3 to 3
- received_sources: int32 [4, 262144], P(None, ('tile', 'rep')), may hold values from 0 to 255, as said below
- recv_counts: int32 [16384, 4], P(('tile', 'rep')), may hold values from 0 to 4, as said below
Outputs:
- snr: float32 [256, 256], P(('tile', 'rep'))
Inputs may be any that keep to these rules, and one draw needn't show every extreme that they name: `received_sources`: entry 0 of a slot is the source the stamp is centred on; the 4 sources of one slot differ. `recv_counts`: in every draw some device receives 4 live slots for one of its blobs from every exposure owner.
All inputs are finite; a program needn't handle non-finite values.
Results may differ from a plain program's by a relative error of at most 0.0032.
Values may be sent and summed in bfloat16 or wider, within the bound.
A program may use at most 64 MiB of HBM per device.

v0:
```python
import functools

import jax
import jax.numpy as jnp
from jax import lax
from jax.experimental import pallas as pl
from jax.experimental.pallas import tpu as pltpu
from jax.sharding import PartitionSpec as P

F32 = jnp.float32
BF16 = jnp.bfloat16
I32 = jnp.int32
HIGHEST = lax.Precision.HIGHEST

PIX = 625
LANES = 128
CHUNKS = 5
PADPIX = CHUNKS * LANES
TILES = 64
REPS = 4
SLOTS = 1024
BASIS = 10
QUAD = 4
CCD = 4
GROUP = 16
GROUPS = TILES // GROUP
GSLOTS = GROUP * 16
GK = GROUP * CCD * BASIS
ORDER = 256
HALF = 128
TERMS = 24
PAIRS = [(q, r) for q in range(QUAD) for r in range(q, QUAD)]
VMEM = pl.BlockSpec(memory_space=pltpu.VMEM)


def iota(shape, axis):
    return lax.broadcasted_iota(I32, shape, axis)


def pack_body(st_ref, cf_ref, iv_ref, cd_ref, put):
    meta = jnp.concatenate(
        [
            cf_ref[...].astype(F32),
            iv_ref[...].astype(F32),
            cd_ref[...].astype(F32),
            jnp.zeros((LANES - QUAD * BASIS - 2, SLOTS), F32),
        ],
        axis=0,
    )
    put(0, jnp.transpose(meta).astype(BF16).reshape(TILES, 16, LANES))
    for chunk in (4, 0, 1, 2, 3):
        if chunk < CHUNKS - 1:
            block = st_ref[chunk * LANES : (chunk + 1) * LANES, :].astype(F32)
        else:
            body = st_ref[chunk * LANES : PIX - 1, :].astype(F32)
            last = jnp.broadcast_to(st_ref[PIX - 1 : PIX, :].astype(F32), (16, SLOTS))
            row = iota((16, SLOTS), 0)
            tail = jnp.where(row == 0, last, jnp.where(row == 1, 1.0, 0.0))
            block = jnp.concatenate([body, tail], axis=0)
        put(chunk + 1, jnp.transpose(block).astype(BF16).reshape(TILES, 16, LANES))


def pack_kernel(st_ref, cf_ref, iv_ref, cd_ref, out_ref):
    def put(index, value):
        out_ref[:, index * 16 : (index + 1) * 16, :] = value

    pack_body(st_ref, cf_ref, iv_ref, cd_ref, put)


def fill_hot(key_ref, hot_ref):
    hot_ref[...] = (iota((SLOTS, SLOTS), 0) == key_ref[...]).astype(F32).astype(BF16)


def stack_kernel(got_ref, key_ref, xt_ref, table_ref, hot_ref):
    fill_hot(key_ref, hot_ref)
    for chunk in range(CHUNKS):
        rows = got_ref[:, (chunk + 1) * 16 : (chunk + 2) * 16, :].reshape(SLOTS, LANES)
        turned = jnp.transpose(rows.astype(F32)).astype(BF16)
        xt_ref[chunk * LANES : (chunk + 1) * LANES, :] = turned
        part = lax.dot_general(
            turned, hot_ref[...], (((1,), (1,)), ((), ())), preferred_element_type=F32
        )
        for blob in range(REPS):
            table_ref[blob, chunk * LANES : (chunk + 1) * LANES, :] = part[
                :, blob * ORDER : (blob + 1) * ORDER
            ].astype(BF16)


def mean_kernel(part_ref, mean_ref):
    total = part_ref[0].astype(F32)
    for g in range(1, REPS):
        total = total + part_ref[g].astype(F32)
    count = total[PIX : PIX + 1, :]
    mean_ref[...] = (total / (1.0 + count)).astype(BF16)


def fill_select(meta, select_ref):
    for h in range(GROUPS):
        cols = meta[:, h * GSLOTS : (h + 1) * GSLOTS]
        row = iota((GK, GSLOTS), 0)
        col = iota((GK, GSLOTS), 1)
        image = row % (CCD * BASIS)
        seen = (row // (CCD * BASIS)) == (col // 16)
        ccd = cols[QUAD * BASIS + 1 : QUAD * BASIS + 2, :]
        hit = seen & ((image // BASIS).astype(F32) == ccd)
        spread_row = iota((GK, LANES), 0) % BASIS
        spread_col = iota((GK, LANES), 1)
        for q in range(QUAD):
            spread = (spread_col == spread_row + q * BASIS).astype(F32).astype(BF16)
            laid = jnp.dot(spread, cols.astype(BF16), preferred_element_type=F32)
            select_ref[h, :, q * GSLOTS : (q + 1) * GSLOTS] = jnp.where(hit, laid, 0.0).astype(BF16)


def render(bases_ref, select_ref, model_ref):
    for h in range(GROUPS):
        image = lax.dot_general(
            bases_ref[h * GK : (h + 1) * GK, :],
            select_ref[h],
            (((0,), (0,)), ((), ())),
            preferred_element_type=F32,
        )
        for q in range(QUAD):
            model_ref[q, :, h * GSLOTS : (h + 1) * GSLOTS] = image[
                :, q * GSLOTS : (q + 1) * GSLOTS
            ].astype(BF16)


def accumulate(chunk, xt_ref, own_ref, model_ref, scale_ref, term_ref, rows=16):
    for lane in range(SLOTS // LANES):
        at = slice(lane * LANES, (lane + 1) * LANES)
        quarter = jnp.broadcast_to(scale_ref[0:1, at], (rows, LANES))
        live = jnp.broadcast_to(scale_ref[1:2, at], (rows, LANES))

        def step(i, sums):
            here = pl.ds(pl.multiple_of(i * rows, rows), rows)
            there = pl.ds(pl.multiple_of(chunk * LANES + i * rows, rows), rows)
            x = xt_ref[there, at].astype(F32)
            gap = x - own_ref[here, at]
            weight = live / (1.0 + quarter * (gap * gap))
            m = [model_ref[q, there, at].astype(F32) for q in range(QUAD)]
            wm = [weight * v for v in m]
            new = [wm[q] * m[r] for q, r in PAIRS] + [wm[q] * x for q in range(QUAD)]
            return tuple(s + v for s, v in zip(sums, new))

        sums = lax.fori_loop(
            0,
            LANES // rows,
            step,
            tuple(jnp.zeros((rows, LANES), F32) for _ in range(14)),
        )
        for n, s in enumerate(sums):
            term_ref[n, :, at] += s[0:8] + s[8:16]


def finish_terms(term_ref, src_ref):
    rows = [jnp.sum(term_ref[n], axis=0, keepdims=True) for n in range(14)]
    block = jnp.concatenate(
        rows + [src_ref[...].astype(F32), jnp.zeros((TERMS - 18, SLOTS), F32)], axis=0
    )
    one = block.astype(BF16)
    rest = block - one.astype(F32)
    two = rest.astype(BF16)
    three = (rest - two.astype(F32)).astype(BF16)
    row = iota((SLOTS, SLOTS), 0)
    col = iota((SLOTS, SLOTS), 1)
    home = ((row // 4) % 4) * ORDER + (row // 16) * 4 + row % 4
    move = (home == col).astype(F32).astype(BF16)
    moved = jnp.dot(jnp.concatenate([one, two, three], axis=0).astype(BF16), move, preferred_element_type=F32)
    return moved[0:TERMS] + moved[TERMS : 2 * TERMS] + moved[2 * TERMS : 3 * TERMS]


def terms_kernel(
    got_ref, xt_ref, mean_ref, key_ref, src_ref, bases_ref, out_ref,
    hot_ref, select_ref, model_ref, scale_ref, own_ref, term_ref,
):
    fill_hot(key_ref, hot_ref)
    meta = jnp.transpose(got_ref[:, 0:16, :].reshape(SLOTS, LANES).astype(F32))
    ivar = meta[QUAD * BASIS : QUAD * BASIS + 1, :]
    scale_ref[0:1, :] = ivar * 0.25
    scale_ref[1:2, :] = jnp.where(key_ref[...] >= 0, ivar, 0.0)
    fill_select(meta, select_ref)
    render(bases_ref, select_ref, model_ref)
    term_ref[...] = jnp.zeros_like(term_ref)
    for chunk in range(CHUNKS):
        at = slice(chunk * LANES, (chunk + 1) * LANES)
        means = jnp.concatenate([mean_ref[b, at, :] for b in range(REPS)], axis=1)
        own_ref[...] = jnp.dot(means, hot_ref[...], preferred_element_type=F32)
        accumulate(chunk, xt_ref, own_ref, model_ref, scale_ref, term_ref)
    block = finish_terms(term_ref, src_ref)
    for b in range(REPS):
        out_ref[b] = block[:, b * ORDER : (b + 1) * ORDER]


def invert(mat_ref):
    lane = iota((8, LANES), 1)
    sub = iota((8, LANES), 0)

    def block(i, _):
        top = pl.multiple_of(i * 8, 8)
        panel = mat_ref[pl.ds(top, 8), :]
        for j in range(8):
            factor = jnp.broadcast_to(panel[:, j : j + 1], (8, LANES))
            row = jnp.broadcast_to(panel[j : j + 1, :], (8, LANES))
            pivot = 1.0 / jnp.broadcast_to(factor[j : j + 1, :], (8, LANES))
            row = jnp.where(lane == j, 1.0, row) * pivot
            kept = jnp.where(lane == j, 0.0, panel)
            panel = jnp.where(sub == j, row, kept - factor * row)
        for n in range(16):
            old = mat_ref[n * 8 : (n + 1) * 8, :]
            new = jnp.where(lane < 8, 0.0, old)
            for j in range(8):
                new = new - jnp.broadcast_to(old[:, j : j + 1], (8, LANES)) * jnp.broadcast_to(
                    panel[j : j + 1, :], (8, LANES)
                )
            new = jnp.where(n == i, panel, new)
            mat_ref[n * 8 : (n + 1) * 8, :] = pltpu.roll(new, LANES - 8, 1)
        return 0

    lax.fori_loop(0, 16, block, 0)


def full(a, b):
    return jnp.dot(a, b, preferred_element_type=F32, precision=HIGHEST)


def solve(terms, work_ref):
    slots = terms.shape[1]
    where = iota((ORDER, slots), 0).astype(F32)
    hot = [where == terms[14 + q : 15 + q, :] for q in range(QUAD)]
    gram = jnp.zeros((ORDER, ORDER), F32)
    rhs = jnp.zeros((ORDER, slots), F32)
    for r in range(QUAD):
        mixed = jnp.zeros((ORDER, slots), F32)
        for q in range(QUAD):
            n = PAIRS.index((min(q, r), max(q, r)))
            mixed = jnp.where(hot[q], terms[n : n + 1, :], mixed)
        high = mixed.astype(BF16)
        low = (mixed - high.astype(F32)).astype(BF16)
        side = hot[r].astype(F32).astype(BF16)
        for part in (high, low):
            gram = gram + lax.dot_general(
                part, side, (((1,), (1,)), ((), ())), preferred_element_type=F32
            )
        rhs = jnp.where(hot[r], terms[10 + r : 11 + r, :], rhs)
    rhs = jnp.sum(rhs, axis=1, keepdims=True)
    eye = iota((ORDER, ORDER), 0) == iota((ORDER, ORDER), 1)
    gram = gram + jnp.where(eye, 1.0, 0.0)
    a12 = gram[:HALF, HALF:]
    a21 = gram[HALF:, :HALF]
    a22 = gram[HALF:, HALF:]
    eye = eye[:HALF, :HALF]

    def turn(col):
        return jnp.transpose(jnp.broadcast_to(col, (HALF, HALF)))[0:1, :]

    r1, r2 = rhs[:HALF], rhs[HALF:]
    work_ref[...] = gram[:HALF, :HALF]
    invert(work_ref)
    top = work_ref[...]
    tie = full(a21, top)
    work_ref[...] = a22 - full(tie, a12)
    invert(work_ref)
    low = work_ref[...]
    v = r2 - jnp.sum(tie * turn(r1), axis=1, keepdims=True)
    f2_row = jnp.sum(low * v, axis=0, keepdims=True)
    f2_col = jnp.sum(low * turn(v), axis=1, keepdims=True)
    f1_row = jnp.sum(top * r1, axis=0, keepdims=True) - jnp.sum(tie * f2_col, axis=0, keepdims=True)
    d2 = jnp.sum(jnp.where(eye, low, 0.0), axis=0, keepdims=True)
    d1 = jnp.sum(jnp.where(eye, top, 0.0), axis=0, keepdims=True) + jnp.sum(
        full(low, tie) * tie, axis=0, keepdims=True
    )
    return f1_row / jnp.sqrt(d1), f2_row / jnp.sqrt(d2)


def solve_kernel(part_ref, out_ref, work_ref):
    terms = jnp.concatenate([part_ref[g] for g in range(REPS)], axis=1)
    left, right = solve(terms, work_ref)
    out_ref[:, :HALF] = left
    out_ref[:, HALF:] = right


def call(kernel, outs, scratch=(), **kw):
    return pl.pallas_call(
        kernel,
        out_shape=outs,
        scratch_shapes=list(scratch),
        **kw,
    )


def struct(shape, dtype):
    return jax.ShapeDtypeStruct(shape, dtype)


def local(stamps, coefs, ivar, ccd, bases, sources, counts):
    pos = jnp.arange(4, dtype=I32)
    live = (pos[None, None, :] < counts[:, :, None]).reshape(1, SLOTS)
    blob = (jnp.arange(SLOTS, dtype=I32) // 4 % 4).reshape(1, SLOTS)
    key = jnp.where(live, sources[0:1] + blob * ORDER, -1)

    mine = jnp.pad(bases.reshape(CCD * BASIS, PIX), ((0, 0), (0, PADPIX - PIX)))
    every = lax.all_gather(mine, "tile", axis=0, tiled=True)

    packed = call(pack_kernel, struct((TILES, 96, LANES), BF16))(
        stamps, coefs.reshape(QUAD * BASIS, SLOTS), ivar.reshape(1, SLOTS), ccd.reshape(1, SLOTS)
    )
    got = lax.all_to_all(packed, "tile", split_axis=0, concat_axis=0, tiled=True)
    turned, tables = call(
        stack_kernel,
        (struct((PADPIX, SLOTS), BF16), struct((REPS, PADPIX, ORDER), BF16)),
        [pltpu.VMEM((SLOTS, SLOTS), BF16)],
    )(got, key)
    parts = lax.all_to_all(tables, "rep", split_axis=0, concat_axis=0, tiled=True)
    mean = call(mean_kernel, struct((PADPIX, ORDER), BF16))(parts)
    means = lax.all_to_all(
        jnp.broadcast_to(mean[None], (REPS, PADPIX, ORDER)), "rep", split_axis=0, concat_axis=0, tiled=True
    )
    terms = call(
        terms_kernel,
        struct((REPS, TERMS, ORDER), F32),
        [
            pltpu.VMEM((SLOTS, SLOTS), BF16),
            pltpu.VMEM((GROUPS, GK, QUAD * GSLOTS), BF16),
            pltpu.VMEM((QUAD, PADPIX, SLOTS), BF16),
            pltpu.VMEM((8, SLOTS), F32),
            pltpu.VMEM((LANES, SLOTS), F32),
            pltpu.VMEM((14, 8, SLOTS), F32),
        ],
    )(got, turned, means, key, sources, every)
    mixed = lax.all_to_all(terms, "rep", split_axis=0, concat_axis=0, tiled=True)
    return call(solve_kernel, struct((1, ORDER), F32), [pltpu.VMEM((HALF, HALF), F32)])(mixed)


def solution(mesh):
    return jax.shard_map(
        local,
        mesh=mesh,
        in_specs=(
            P(None, ("tile", "rep")),
            P(None, None, ("tile", "rep")),
            P(("tile", "rep")),
            P(("tile", "rep")),
            P(("tile", "rep"), None, None),
            P(None, ("tile", "rep")),
            P(("tile", "rep"), None),
        ),
        out_specs=P(("tile", "rep"), None),
        check_vma=False,
    )
```

profile of v0, /device:TPU:2, one launch (start us, length us, event | category | flops | bytes accessed | tf_op | source)
XLA Modules:
  0.0 197.6 jit_solution(17404721454027695593)
XLA Ops:
  6.5 0.0 all-gather.2.cloned.1.call-start
  6.5 0.8 copy.13
  7.4 0.6 pad.4
  8.0 0.0 all-gather.2.cloned.1.call-update
  8.0 0.9 copy.11
  9.0 0.7 reshape.109.cf_ref
  9.6 1.3 reshape.110.iv_ref
  10.9 3.0 %shard_map.73 = bf16[64,96,128]{2,1,0:T(8,128)(2,1)} custom-call(bf16[625,1024]{1,0:T(8,128)(2,1)} %st_ref.1, bf16[40,1024]{1,0:T(8,128)(2,1)} %reshape.109.cf_ref, bf16[1,1024]{1,0:T(2,128)(2,1)} %reshape.110.iv_ref, s32[1,1024]{1,0:T(1,128)} %bitcast.1), custom_call_target="tpu_custom_call" | custom-call | tf_op jit(solution)/shard_map/pallas_call | solution.py:304
  13.9 0.0 copy-start.1
  13.9 12.2 %all-to-all-start = ((bf16[64,96,128]{2,1,0:T(8,128)(2,1)}), bf16[64,96,128]{2,1,0:T(8,128)(2,1)S(1)}, u32[]{:S(2)}, u32[]{:S(2)}) async-start(bf16[64,96,128]{2,1,0:T(8,128)(2,1)} %shard_map.73), calls=%async_computation | async-start | bytes 3145728 | tf_op jit(solution)/shard_map/all_to_all | solution.py:307
  26.1 0.0 copy-done.1
  26.1 0.1 copy.12
  26.2 0.1 iota_compare_fusion
  26.3 0.1 lt.32
  26.4 1.3 fusion.2.key_ref
  27.8 38.9 %all-to-all-done.got_ref = bf16[64,96,128]{2,1,0:T(8,128)(2,1)S(1)} async-done(((bf16[64,96,128]{2,1,0:T(8,128)(2,1)}), bf16[64,96,128]{2,1,0:T(8,128)(2,1)S(1)}, u32[]{:S(2)}, u32[]{:S(2)}) %all-to-all-start) | async-done | bytes 1572896 | tf_op jit(solution)/shard_map/all_to_all | solution.py:307
  66.6 0.0 copy-start
  66.6 1.1 copy-done
  67.8 6.1 %shard_map.74 = (bf16[640,1024]{1,0:T(8,128)(2,1)}, bf16[4,640,256]{2,1,0:T(8,128)(2,1)}) custom-call(bf16[64,96,128]{2,1,0:T(8,128)(2,1)} %copy-done, s32[1,1024]{1,0:T(1,128)} %fusion.2.key_ref), custom_call_target="tpu_custom_call" | custom-call | tf_op jit(solution)/shard_map/pallas_call | solution.py:308
  73.9 23.9 %all_to_all.20.part_ref = bf16[4,640,256]{2,1,0:T(8,128)(2,1)} all-to-all(bf16[4,640,256]{2,1,0:T(8,128)(2,1)} %get-tuple-element.8), channel_id=1, replica_groups=mesh['tile'=64,'rep'=4] {'rep'}, dimensions={0} | all-to-all | bytes 2621440 | tf_op jit(solution)/shard_map/all_to_all | solution.py:313
  97.7 2.2 %shard_map.75 = bf16[640,256]{1,0:T(8,128)(2,1)} custom-call(bf16[4,640,256]{2,1,0:T(8,128)(2,1)} %all_to_all.20.part_ref), custom_call_target="tpu_custom_call" | custom-call | tf_op jit(solution)/shard_map/pallas_call | solution.py:314
  100.0 1.1 broadcast_in_dim.4
  101.0 21.6 %all_to_all.21.mean_ref = bf16[4,640,256]{2,1,0:T(8,128)(2,1)} all-to-all(bf16[4,640,256]{2,1,0:T(8,128)(2,1)S(1)} %broadcast_in_dim.4), channel_id=1, replica_groups=mesh['tile'=64,'rep'=4] {'rep'}, dimensions={0} | all-to-all | bytes 2621440 | tf_op jit(solution)/shard_map/all_to_all | solution.py:315
  122.6 0.0 all-gather.2.cloned.1.call-done.bases_ref
  122.6 22.3 %shard_map.76 = f32[4,24,256]{2,1,0:T(8,128)} custom-call(bf16[64,96,128]{2,1,0:T(8,128)(2,1)} %copy-done, bf16[640,1024]{1,0:T(8,128)(2,1)} %get-tuple-element.7.xt_ref, bf16[4,640,256]{2,1,0:T(8,128)(2,1)} %all_to_all.21.mean_ref, s32[1,1024]{1,0:T(1,128)} %fusion.2.key_ref, s32[4,1024]{1,0:T(4,128)} %src_ref.1, ...), custom_call_target="tpu_custom_call" | custom-call | tf_op jit(solution)/shard_map/pallas_call | solution.py:318
  145.0 9.8 %all_to_all.22.part_ref = f32[4,24,256]{2,1,0:T(8,128)} all-to-all(f32[4,24,256]{2,1,0:T(8,128)} %shard_map.76), channel_id=1, replica_groups=mesh['tile'=64,'rep'=4] {'rep'}, dimensions={0} | all-to-all | bytes 196608 | tf_op jit(solution)/shard_map/all_to_all | solution.py:330
  154.7 36.0 %shard_map.77 = f32[1,256]{1,0:T(1,128)} custom-call(f32[4,24,256]{2,1,0:T(8,128)} %all_to_all.22.part_ref), custom_call_target="tpu_custom_call" | custom-call | tf_op jit(solution)/shard_map/pallas_call | solution.py:331
  (1 shorter events, 0.0 us)
Async XLA Ops:
  6.5 116.1 %all-gather.2.cloned.1.call-start = ((), (), s32[]{:S(2)}) async-start(), calls=%async_computation.4 | async-start | bytes 3328000 | tf_op jit(solution)/shard_map/all_gather | solution.py:302
  13.9 12.2 %copy-start.1 = (s32[64,4]{0,1:T(4,128)S(1)}, s32[64,4]{0,1:T(4,128)}, u32[]{:S(2)}) copy-start(s32[64,4]{0,1:T(4,128)} %param.13) | copy-start | bytes 3076
  13.9 52.7 %all-to-all-start = ((bf16[64,96,128]{2,1,0:T(8,128)(2,1)}), bf16[64,96,128]{2,1,0:T(8,128)(2,1)S(1)}, u32[]{:S(2)}, u32[]{:S(2)}) async-start(bf16[64,96,128]{2,1,0:T(8,128)(2,1)} %shard_map.73), calls=%async_computation | async-start | bytes 3145728 | tf_op jit(solution)/shard_map/all_to_all | solution.py:307
  66.6 1.1 copy-start
Sparse Core Ops, SparseCore 0:
  10.0 81.3 all-gather.1
where the time goes:
time: 198 us
  Pallas kernels  69.6 us (35%)
  blocking collectives  55.3 us (28%)
  waiting for transfers between devices  38.9 us (20%)
  between operations  13.4 us (7%)
  starting transfers between devices  12.2 us (6%)
  local copies, waits for them, and re-layouts  6.77 us (3%)
    all_to_all x1, waiting for transfers between devices, local(): lax.all_to_all(packed, 'tile', split_axis=0, concat_axis=0, tiled=True)  38.9 us
    pallas_call x1, Pallas kernels, local(): call(solve_kernel, struct((1, ORDER), F32), [pltpu.VMEM((HALF, HALF), F32)])  36 us
    all_to_all x1, blocking collectives, local(): lax.all_to_all(tables, 'rep', split_axis=0, concat_axis=0, tiled=True)  23.9 us
    pallas_call x1, Pallas kernels, local(): call(terms_kernel, struct((REPS, TERMS, ORDER), F32), [pltpu.VMEM((SLOTS,...  22.3 us
    all_to_all x1, blocking collectives, local(): lax.all_to_all(jnp.broadcast_to(mean[None], (REPS, PADPIX, ORDER)), 'rep'...  21.6 us
    all_to_all x1, starting transfers between devices, local(): lax.all_to_all(packed, 'tile', split_axis=0, concat_axis=0, tiled=True)  12.2 us
    all_to_all x1, blocking collectives, local(): lax.all_to_all(terms, 'rep', split_axis=0, concat_axis=0, tiled=True)  9.78 us
    pallas_call x1, Pallas kernels, local(): call(stack_kernel, (struct((PADPIX, SLOTS), BF16), struct((REPS, PADPIX,...  6.06 us
  transfers between devices with their start and end apart: 2, of which 1 were waited for; matrix products, arithmetic and copies ran while one was open for 3% of the time, Pallas kernels for 6%

commit v1 on v0

--- a/solution.py
+++ b/solution.py
@@ -25,11 +25,13 @@
 GROUP = 16
 GROUPS = TILES // GROUP
 GSLOTS = GROUP * 16
-GK = GROUP * CCD * BASIS
+ROWS = 48
+GK = GROUP * ROWS
 ORDER = 256
 HALF = 128
 TERMS = 24
 PAIRS = [(q, r) for q in range(QUAD) for r in range(q, QUAD)]
+MESH = pl.DeviceIdType.MESH
 VMEM = pl.BlockSpec(memory_space=pltpu.VMEM)
 
 
@@ -37,18 +39,21 @@
     return lax.broadcasted_iota(I32, shape, axis)
 
 
-def pack_body(st_ref, cf_ref, iv_ref, cd_ref, put):
-    meta = jnp.concatenate(
-        [
-            cf_ref[...].astype(F32),
-            iv_ref[...].astype(F32),
-            cd_ref[...].astype(F32),
-            jnp.zeros((LANES - QUAD * BASIS - 2, SLOTS), F32),
-        ],
-        axis=0,
-    )
-    put(0, jnp.transpose(meta).astype(BF16).reshape(TILES, 16, LANES))
-    for chunk in (4, 0, 1, 2, 3):
+def pack_body(st_ref, cf_ref, iv_ref, cd_ref, put, which):
+    if 0 in which:
+        meta = jnp.concatenate(
+            [
+                cf_ref[...].astype(F32),
+                iv_ref[...].astype(F32),
+                cd_ref[...].astype(F32),
+                jnp.zeros((LANES - QUAD * BASIS - 2, SLOTS), F32),
+            ],
+            axis=0,
+        )
+        put(0, jnp.transpose(meta).astype(BF16).reshape(TILES, 16, LANES))
+    for chunk in range(CHUNKS):
+        if chunk + 1 not in which:
+            continue
         if chunk < CHUNKS - 1:
             block = st_ref[chunk * LANES : (chunk + 1) * LANES, :].astype(F32)
         else:
@@ -60,38 +65,8 @@
         put(chunk + 1, jnp.transpose(block).astype(BF16).reshape(TILES, 16, LANES))
 
 
-def pack_kernel(st_ref, cf_ref, iv_ref, cd_ref, out_ref):
-    def put(index, value):
-        out_ref[:, index * 16 : (index + 1) * 16, :] = value
-
-    pack_body(st_ref, cf_ref, iv_ref, cd_ref, put)
-
-
 def fill_hot(key_ref, hot_ref):
     hot_ref[...] = (iota((SLOTS, SLOTS), 0) == key_ref[...]).astype(F32).astype(BF16)
-
-
-def stack_kernel(got_ref, key_ref, xt_ref, table_ref, hot_ref):
-    fill_hot(key_ref, hot_ref)
-    for chunk in range(CHUNKS):
-        rows = got_ref[:, (chunk + 1) * 16 : (chunk + 2) * 16, :].reshape(SLOTS, LANES)
-        turned = jnp.transpose(rows.astype(F32)).astype(BF16)
-        xt_ref[chunk * LANES : (chunk + 1) * LANES, :] = turned
-        part = lax.dot_general(
-            turned, hot_ref[...], (((1,), (1,)), ((), ())), preferred_element_type=F32
-        )
-        for blob in range(REPS):
-            table_ref[blob, chunk * LANES : (chunk + 1) * LANES, :] = part[
-                :, blob * ORDER : (blob + 1) * ORDER
-            ].astype(BF16)
-
-
-def mean_kernel(part_ref, mean_ref):
-    total = part_ref[0].astype(F32)
-    for g in range(1, REPS):
-        total = total + part_ref[g].astype(F32)
-    count = total[PIX : PIX + 1, :]
-    mean_ref[...] = (total / (1.0 + count)).astype(BF16)
 
 
 def fill_select(meta, select_ref):
@@ -99,11 +74,11 @@
         cols = meta[:, h * GSLOTS : (h + 1) * GSLOTS]
         row = iota((GK, GSLOTS), 0)
         col = iota((GK, GSLOTS), 1)
-        image = row % (CCD * BASIS)
-        seen = (row // (CCD * BASIS)) == (col // 16)
+        image = row % ROWS
+        seen = (row // ROWS) == (col // 16)
         ccd = cols[QUAD * BASIS + 1 : QUAD * BASIS + 2, :]
         hit = seen & ((image // BASIS).astype(F32) == ccd)
-        spread_row = iota((GK, LANES), 0) % BASIS
+        spread_row = (iota((GK, LANES), 0) % ROWS) % BASIS
         spread_col = iota((GK, LANES), 1)
         for q in range(QUAD):
             spread = (spread_col == spread_row + q * BASIS).astype(F32).astype(BF16)
@@ -111,10 +86,10 @@
             select_ref[h, :, q * GSLOTS : (q + 1) * GSLOTS] = jnp.where(hit, laid, 0.0).astype(BF16)
 
 
-def render(bases_ref, select_ref, model_ref):
+def render(every_ref, select_ref, model_ref):
     for h in range(GROUPS):
         image = lax.dot_general(
-            bases_ref[h * GK : (h + 1) * GK, :],
+            every_ref[h * 8 : (h + 1) * 8].reshape(GK, PADPIX),
             select_ref[h],
             (((0,), (0,)), ((), ())),
             preferred_element_type=F32,
@@ -167,28 +142,6 @@
     move = (home == col).astype(F32).astype(BF16)
     moved = jnp.dot(jnp.concatenate([one, two, three], axis=0).astype(BF16), move, preferred_element_type=F32)
     return moved[0:TERMS] + moved[TERMS : 2 * TERMS] + moved[2 * TERMS : 3 * TERMS]
-
-
-def terms_kernel(
-    got_ref, xt_ref, mean_ref, key_ref, src_ref, bases_ref, out_ref,
-    hot_ref, select_ref, model_ref, scale_ref, own_ref, term_ref,
-):
-    fill_hot(key_ref, hot_ref)
-    meta = jnp.transpose(got_ref[:, 0:16, :].reshape(SLOTS, LANES).astype(F32))
-    ivar = meta[QUAD * BASIS : QUAD * BASIS + 1, :]
-    scale_ref[0:1, :] = ivar * 0.25
-    scale_ref[1:2, :] = jnp.where(key_ref[...] >= 0, ivar, 0.0)
-    fill_select(meta, select_ref)
-    render(bases_ref, select_ref, model_ref)
-    term_ref[...] = jnp.zeros_like(term_ref)
-    for chunk in range(CHUNKS):
-        at = slice(chunk * LANES, (chunk + 1) * LANES)
-        means = jnp.concatenate([mean_ref[b, at, :] for b in range(REPS)], axis=1)
-        own_ref[...] = jnp.dot(means, hot_ref[...], preferred_element_type=F32)
-        accumulate(chunk, xt_ref, own_ref, model_ref, scale_ref, term_ref)
-    block = finish_terms(term_ref, src_ref)
-    for b in range(REPS):
-        out_ref[b] = block[:, b * ORDER : (b + 1) * ORDER]
 
 
 def invert(mat_ref):
@@ -272,20 +225,196 @@
     return f1_row / jnp.sqrt(d1), f2_row / jnp.sqrt(d2)
 
 
-def solve_kernel(part_ref, out_ref, work_ref):
-    terms = jnp.concatenate([part_ref[g] for g in range(REPS)], axis=1)
-    left, right = solve(terms, work_ref)
+def remote(src, dst, send, recv, **where):
+    return pltpu.make_async_remote_copy(
+        src_ref=src, dst_ref=dst, send_sem=send, recv_sem=recv, device_id=where, device_id_type=MESH
+    )
+
+
+def whole_kernel(
+    st_ref, cf_ref, iv_ref, cd_ref, key_ref, src_ref, mine_ref, out_ref,
+    packed, got, every, xt_ref, hot_ref, select_ref, model_ref, scale_ref, own_ref, term_ref,
+    tables, parts, mean_own, means, count_ref, terms_out, terms_in, work_ref,
+    a_send, a_recv, b_send, b_recv, t_send, t_recv, m_send, m_recv, e_send, e_recv,
+):
+    me = lax.axis_index("tile")
+    g = lax.axis_index("rep")
+    x, z, c = me // 16, (me // 2) % 8, me % 2
+
+    def peer(dx, dz, core):
+        return (((x + dx + 4) % 4) * 8 + (z + dz + 8) % 8) * 2 + core
+
+    barrier = pltpu.get_barrier_semaphore()
+
+    def greet(o, _):
+        pl.semaphore_signal(barrier, inc=1, device_id={"tile": (me + o) % TILES}, device_id_type=MESH)
+        return 0
+
+    lax.fori_loop(1, TILES, greet, 0)
+    for d in range(1, REPS):
+        pl.semaphore_signal(barrier, inc=1, device_id={"rep": (g + d) % REPS}, device_id_type=MESH)
+
+    def send_block(n):
+        def one(o, _):
+            p = (me + o) % TILES
+            remote(packed.at[n, p], got.at[n, me], a_send.at[n], a_recv.at[n], tile=p).start()
+            return 0
+
+        lax.fori_loop(1, TILES, one, 0)
+        got[n, pl.ds(me, 1)] = packed[n, pl.ds(me, 1)]
+
+    def block_done(n):
+        many = pl.ds(0, TILES - 1)
+        return remote(packed.at[n, many], got.at[n, many], a_send.at[n], a_recv.at[n], tile=peer(0, 1, c))
+
+    def blocks_done(stage, count):
+        many = every.at[pl.ds(0, count), 0]
+        return remote(many, many, b_send.at[stage], b_recv.at[stage], tile=peer(0, 1, c))
+
+    def send_bases(stage, ref, dx, dz, core):
+        remote(ref, ref, b_send.at[stage], b_recv.at[stage], tile=peer(dx, dz, core)).start()
+
+    here = x * 8 + z
+
+    def pack(n):
+        def put(index, value):
+            packed[index] = value
+
+        pack_body(st_ref, cf_ref, iv_ref, cd_ref, put, (n,))
+
+    def stage_z1():
+        for dz in (1, -1, 2, -2):
+            remote(
+                mine_ref, every.at[here, c], b_send.at[0], b_recv.at[0], tile=peer(0, dz, c)
+            ).start()
+
+    def stage_z2():
+        blocks_done(0, 4).wait_recv()
+        low = every.at[x * 8 + (z + 6) % 8, c]
+        high = every.at[x * 8 + (z + 2) % 8, c]
+        send_bases(1, low, 0, 1, c)
+        send_bases(1, high, 0, -1, c)
+        send_bases(1, low, 0, 2, c)
+
+    def stage_x1():
+        blocks_done(1, 3).wait_recv()
+        column = every.at[pl.ds(x * 8, 8), c]
+        send_bases(2, column, 1, 0, c)
+        send_bases(2, column, -1, 0, c)
+
+    def stage_x2():
+        blocks_done(2, 16).wait_recv()
+        send_bases(3, every.at[pl.ds(((x + 3) % 4) * 8, 4), c], 1, 0, c)
+        send_bases(3, every.at[pl.ds(((x + 1) % 4) * 8 + 4, 4), c], -1, 0, c)
+
+    def stage_core():
+        blocks_done(3, 8).wait_recv()
+        send_bases(4, every.at[pl.ds(0, 32), c], 0, 0, 1 - c)
+
+    def stack(n):
+        block_done(n + 1).wait_recv()
+        turned = jnp.transpose(got[n + 1].reshape(SLOTS, LANES).astype(F32)).astype(BF16)
+        xt_ref[n * LANES : (n + 1) * LANES, :] = turned
+        part = lax.dot_general(
+            turned, hot_ref[...], (((1,), (1,)), ((), ())), preferred_element_type=F32
+        )
+        for b in range(REPS):
+            tables[n, b] = part[:, b * ORDER : (b + 1) * ORDER].astype(BF16)
+        for d in range(1, REPS):
+            b = (g + d) % REPS
+            remote(tables.at[n, b], parts.at[n, g], t_send.at[n], t_recv.at[n], rep=b).start()
+        parts[n, pl.ds(g, 1)] = tables[n, pl.ds(g, 1)]
+
+    def three(src, dst, send, recv, n):
+        many = pl.ds(0, REPS - 1)
+        return remote(src.at[n, many], dst.at[n, many], send.at[n], recv.at[n], rep=(g + 1) % REPS)
+
+    def mean(n):
+        three(tables, parts, t_send, t_recv, n).wait_recv()
+        total = parts[n, 0].astype(F32)
+        for other in range(1, REPS):
+            total = total + parts[n, other].astype(F32)
+        if n == CHUNKS - 1:
+            at = PIX - (CHUNKS - 1) * LANES
+            count_ref[...] = jnp.broadcast_to(total[at : at + 1, :], (8, ORDER))
+        value = (total / (1.0 + count_ref[0:1, :])).astype(BF16)
+        mean_own[n, 0] = value
+        for d in range(1, REPS):
+            remote(
+                mean_own.at[n, 0], means.at[n, g], m_send.at[n], m_recv.at[n], rep=(g + d) % REPS
+            ).start()
+        means[n, pl.ds(g, 1)] = mean_own[n]
+
+    def terms(n):
+        three(means, means, m_send, m_recv, n).wait_recv()
+        joined = jnp.concatenate([means[n, b] for b in range(REPS)], axis=1)
+        own_ref[...] = jnp.dot(joined, hot_ref[...], preferred_element_type=F32)
+        accumulate(n, xt_ref, own_ref, model_ref, scale_ref, term_ref)
+
+    pack(0)
+    pack(5)
+    every[pl.ds(here, 1), pl.ds(c, 1)] = mine_ref[...].reshape(1, 1, ROWS, PADPIX)
+    pl.semaphore_wait(barrier, TILES - 1 + REPS - 1)
+    stage_z1()
+    send_block(0)
+    send_block(5)
+    pack(1)
+    send_block(1)
+    stage_z2()
+    pack(2)
+    send_block(2)
+    fill_hot(key_ref, hot_ref)
+    term_ref[...] = jnp.zeros_like(term_ref)
+    stage_x1()
+    pack(3)
+    send_block(3)
+    block_done(0).wait_recv()
+    meta = jnp.transpose(got[0].reshape(SLOTS, LANES).astype(F32))
+    ivar = meta[QUAD * BASIS : QUAD * BASIS + 1, :]
+    scale_ref[0:1, :] = ivar * 0.25
+    scale_ref[1:2, :] = jnp.where(key_ref[...] >= 0, ivar, 0.0)
+    stage_x2()
+    pack(4)
+    send_block(4)
+    fill_select(meta, select_ref)
+    stack(4)
+    stage_core()
+    stack(0)
+    mean(4)
+    stack(1)
+    mean(0)
+    blocks_done(4, 32).wait_recv()
+    render(every, select_ref, model_ref)
+    terms(4)
+    stack(2)
+    mean(1)
+    terms(0)
+    stack(3)
+    mean(2)
+    terms(1)
+    mean(3)
+    terms(2)
+    terms(3)
+    block = finish_terms(term_ref, src_ref)
+    for b in range(REPS):
+        terms_out[0, b] = block[:, b * ORDER : (b + 1) * ORDER]
+    for d in range(1, REPS):
+        b = (g + d) % REPS
+        remote(terms_out.at[0, b], terms_in.at[0, g], e_send.at[0], e_recv.at[0], rep=b).start()
+    terms_in[0, pl.ds(g, 1)] = terms_out[0, pl.ds(g, 1)]
+    three(terms_out, terms_in, e_send, e_recv, 0).wait_recv()
+    left, right = solve(jnp.concatenate([terms_in[0, k] for k in range(REPS)], axis=1), work_ref)
     out_ref[:, :HALF] = left
     out_ref[:, HALF:] = right
 
-
-def call(kernel, outs, scratch=(), **kw):
-    return pl.pallas_call(
-        kernel,
-        out_shape=outs,
-        scratch_shapes=list(scratch),
-        **kw,
-    )
+    for n in range(CHUNKS + 1):
+        block_done(n).wait_send()
+    for stage, count in enumerate((4, 3, 16, 8, 32)):
+        blocks_done(stage, count).wait_send()
+    for n in range(CHUNKS):
+        three(tables, parts, t_send, t_recv, n).wait_send()
+        three(means, means, m_send, m_recv, n).wait_send()
+    three(terms_out, terms_in, e_send, e_recv, 0).wait_send()
 
 
 def struct(shape, dtype):
@@ -297,38 +426,57 @@
     live = (pos[None, None, :] < counts[:, :, None]).reshape(1, SLOTS)
     blob = (jnp.arange(SLOTS, dtype=I32) // 4 % 4).reshape(1, SLOTS)
     key = jnp.where(live, sources[0:1] + blob * ORDER, -1)
-
-    mine = jnp.pad(bases.reshape(CCD * BASIS, PIX), ((0, 0), (0, PADPIX - PIX)))
-    every = lax.all_gather(mine, "tile", axis=0, tiled=True)
-
-    packed = call(pack_kernel, struct((TILES, 96, LANES), BF16))(
-        stamps, coefs.reshape(QUAD * BASIS, SLOTS), ivar.reshape(1, SLOTS), ccd.reshape(1, SLOTS)
-    )
-    got = lax.all_to_all(packed, "tile", split_axis=0, concat_axis=0, tiled=True)
-    turned, tables = call(
-        stack_kernel,
-        (struct((PADPIX, SLOTS), BF16), struct((REPS, PADPIX, ORDER), BF16)),
-        [pltpu.VMEM((SLOTS, SLOTS), BF16)],
-    )(got, key)
-    parts = lax.all_to_all(tables, "rep", split_axis=0, concat_axis=0, tiled=True)
-    mean = call(mean_kernel, struct((PADPIX, ORDER), BF16))(parts)
-    means = lax.all_to_all(
-        jnp.broadcast_to(mean[None], (REPS, PADPIX, ORDER)), "rep", split_axis=0, concat_axis=0, tiled=True
-    )
-    terms = call(
-        terms_kernel,
-        struct((REPS, TERMS, ORDER), F32),
-        [
+    mine = jnp.pad(
+        bases.reshape(CCD * BASIS, PIX), ((0, ROWS - CCD * BASIS), (0, PADPIX - PIX))
+    )
+    dma = pltpu.SemaphoreType.DMA
+    return pl.pallas_call(
+        whole_kernel,
+        out_shape=struct((1, ORDER), F32),
+        in_specs=[VMEM] * 7,
+        out_specs=VMEM,
+        scratch_shapes=[
+            pltpu.VMEM((CHUNKS + 1, TILES, 16, LANES), BF16),
+            pltpu.VMEM((CHUNKS + 1, TILES, 16, LANES), BF16),
+            pltpu.VMEM((32, 2, ROWS, PADPIX), BF16),
+            pltpu.VMEM((PADPIX, SLOTS), BF16),
             pltpu.VMEM((SLOTS, SLOTS), BF16),
             pltpu.VMEM((GROUPS, GK, QUAD * GSLOTS), BF16),
             pltpu.VMEM((QUAD, PADPIX, SLOTS), BF16),
             pltpu.VMEM((8, SLOTS), F32),
             pltpu.VMEM((LANES, SLOTS), F32),
             pltpu.VMEM((14, 8, SLOTS), F32),
+            pltpu.VMEM((CHUNKS, REPS, LANES, ORDER), BF16),
+            pltpu.VMEM((CHUNKS, REPS, LANES, ORDER), BF16),
+            pltpu.VMEM((CHUNKS, 1, LANES, ORDER), BF16),
+            pltpu.VMEM((CHUNKS, REPS, LANES, ORDER), BF16),
+            pltpu.VMEM((8, ORDER), F32),
+            pltpu.VMEM((1, REPS, TERMS, ORDER), F32),
+            pltpu.VMEM((1, REPS, TERMS, ORDER), F32),
+            pltpu.VMEM((HALF, HALF), F32),
+            dma((CHUNKS + 1,)),
+            dma((CHUNKS + 1,)),
+            dma((5,)),
+            dma((5,)),
+            dma((CHUNKS,)),
+            dma((CHUNKS,)),
+            dma((CHUNKS,)),
+            dma((CHUNKS,)),
+            dma((1,)),
+            dma((1,)),
         ],
-    )(got, turned, means, key, sources, every)
-    mixed = lax.all_to_all(terms, "rep", split_axis=0, concat_axis=0, tiled=True)
-    return call(solve_kernel, struct((1, ORDER), F32), [pltpu.VMEM((HALF, HALF), F32)])(mixed)
+        compiler_params=pltpu.CompilerParams(
+            collective_id=0, has_side_effects=True, vmem_limit_bytes=60 * 1024 * 1024
+        ),
+    )(
+        stamps,
+        coefs.reshape(QUAD * BASIS, SLOTS),
+        ivar.reshape(1, SLOTS),
+        ccd.reshape(1, SLOTS),
+        key,
+        sources,
+        mine,
+    )
 
 
 def solution(mesh):

time: 198 us -> 146 us (0.74)
  Pallas kernels: 69.6 us -> 137 us
  blocking collectives: 55.3 us -> 0 us
  waiting for transfers between devices: 38.9 us -> 0 us
  between operations: 13.4 us -> 0.03 us
  starting transfers between devices: 12.2 us -> 0 us
    pallas_call x5 -> x1, Pallas kernels: 69.6 us -> 137 us  [local(): pl.pallas_call(whole_kernel, out_shape=struct((1, ORDER), F32), in_specs=...]
    all_to_all x3 -> x0, blocking collectives: 55.3 us -> none  [the longest x1 23.9 us: local(): lax.all_to_all(tables, 'rep', split_axis=0, concat_axis=0, tiled=True)]
    all_to_all x1 -> x0, waiting for transfers between devices: 38.9 us -> none  [local(): lax.all_to_all(packed, 'tile', split_axis=0, concat_axis=0, tiled=True)]
    all_to_all x1 -> x0, starting transfers between devices: 12.2 us -> none  [local(): lax.all_to_all(packed, 'tile', split_axis=0, concat_axis=0, tiled=True)]
  transfers between devices with their start and end apart: 2 -> 0, of which waited for: 1 -> 0; matrix products, arithmetic and copies ran while one was open for 3% -> 0% of each run, Pallas kernels for 6% -> 0%
where the time goes in v1:
time: 146 us; the launch traced here: 144 us
  Pallas kernels  137 us (94%)
  local copies, waits for them, and re-layouts  6.44 us (4%)
  other arithmetic  1.46 us (1%)
    pallas_call x1, Pallas kernels, local(): pl.pallas_call(whole_kernel, out_shape=struct((1, ORDER), F32), in_specs=...  137 us
    unnamed x4, local copies, waits for them, and re-layouts  3.7 us

profile of v1, /device:TPU:2, one launch (start us, length us, event | category | flops | bytes accessed | tf_op | source)
XLA Modules:
  0.0 144.5 jit_solution(15765779145357125449)
XLA Ops:
  0.0 0.9 copy.11
  0.9 0.7 reshape.108.cf_ref
  1.6 0.8 copy.13
  2.4 0.6 pad.4.mine_ref
  3.1 0.8 copy.12
  3.8 0.1 iota_compare_fusion
  4.0 0.1 lt.32
  4.1 1.3 fusion.2.key_ref
  5.4 1.3 reshape.109.iv_ref
  6.7 136.6 %shard_map.73 = f32[1,256]{1,0:T(1,128)} custom-call(bf16[625,1024]{1,0:T(8,128)(2,1)} %st_ref.1, bf16[40,1024]{1,0:T(8,128)(2,1)} %reshape.108.cf_ref, bf16[1,1024]{1,0:T(2,128)(2,1)} %reshape.109.iv_ref, s32[1,1024]{1,0:T(1,128)} %bitcast.1, s32[1,1024]{1,0:T(1,128)} %fusion.2.key_ref, s32[4,1024]{1,0:T(4,128)} %src_ref.1, bf16[48,640]{1,0:T(8,128)(2,1)} %pad.4.mine_ref), custom_call_target="tpu_custom_call" | custom-call | tf_op jit(solution)/shard_map/pallas_call | solution.py:433
  143.3 1.2 copy.15
  (1 shorter events, 0.0 us)

commit v2 on v1

v2 whole, which is shorter than its diff:
```python
import functools

import jax
import jax.numpy as jnp
from jax import lax
from jax.experimental import pallas as pl
from jax.experimental.pallas import tpu as pltpu
from jax.sharding import PartitionSpec as P

F32 = jnp.float32
BF16 = jnp.bfloat16
I32 = jnp.int32
HIGHEST = lax.Precision.HIGHEST

PIX = 625
LANES = 128
CHUNKS = 5
PADPIX = CHUNKS * LANES
TILES = 64
REPS = 4
SLOTS = 1024
BASIS = 10
QUAD = 4
CCD = 4
GROUP = 16
GROUPS = TILES // GROUP
GSLOTS = GROUP * 16
ROWS = 48
GK = GROUP * ROWS
ORDER = 256
HALF = 128
TERMS = 16
UNROLL = 2
PAIRS = [(q, r) for q in range(QUAD) for r in range(q, QUAD)]
MESH = pl.DeviceIdType.MESH
VMEM = pl.BlockSpec(memory_space=pltpu.VMEM)


def iota(shape, axis):
    return lax.broadcasted_iota(I32, shape, axis)


def flat(ref):
    return jnp.concatenate([ref[i : i + 1, :].astype(F32) for i in range(8)], axis=1)


def pack_meta(cf_ref, iv_ref, cd_ref, out_ref):
    meta = jnp.concatenate(
        [cf_ref[k].astype(F32) for k in range(BASIS)]
        + [flat(iv_ref), flat(cd_ref), jnp.zeros((LANES - QUAD * BASIS - 2, SLOTS), F32)],
        axis=0,
    )
    rows = jnp.transpose(meta).reshape(TILES, 16, LANES)
    left = rows[:, :8].reshape(TILES * 8, LANES)
    right = rows[:, 8:].reshape(TILES * 8, LANES)
    out_ref[...] = (left + pltpu.roll(right, 64, 1)).reshape(TILES, 8, LANES).astype(BF16)


def unpack_meta(got_ref):
    rows = got_ref[...].astype(F32)
    other = pltpu.roll(rows.reshape(TILES * 8, LANES), 64, 1).reshape(TILES, 8, LANES)
    return jnp.transpose(jnp.concatenate([rows, other], axis=1).reshape(SLOTS, LANES))


def pack_block(st_ref, chunk, out_ref):
    if chunk < CHUNKS - 1:
        block = st_ref[chunk * LANES : (chunk + 1) * LANES, :].astype(F32)
    else:
        body = st_ref[chunk * LANES : PIX - 1, :].astype(F32)
        last = jnp.broadcast_to(st_ref[PIX - 1 : PIX, :].astype(F32), (16, SLOTS))
        row = iota((16, SLOTS), 0)
        tail = jnp.where(row == 0, last, jnp.where(row == 1, 1.0, 0.0))
        block = jnp.concatenate([body, tail], axis=0)
    out_ref[chunk] = jnp.transpose(block).astype(BF16).reshape(TILES, 16, LANES)


def fill_key(counts_ref, src_ref, key_ref):
    owner = (iota((TILES, SLOTS), 0) == iota((TILES, SLOTS), 1) // 16).astype(F32).astype(BF16)
    count = jnp.concatenate(
        [counts_ref[...].astype(F32), jnp.zeros((12, TILES), F32)], axis=0
    ).astype(BF16)
    laid = jnp.dot(count, owner, preferred_element_type=F32)
    lane = iota((1, SLOTS), 1)
    blob = (lane // 4) % 4
    mine = jnp.zeros((1, SLOTS), F32)
    for b in range(REPS):
        mine = jnp.where(blob == b, laid[b : b + 1, :], mine)
    live = (lane % 4).astype(F32) < mine
    key_ref[...] = jnp.where(live, src_ref[0:1, :] + blob * ORDER, -1)


def fill_move(move_ref):
    row = iota((SLOTS, 1), 0)
    home = ((row // 4) % 4) * ORDER + (row // 16) * 4 + row % 4
    move_ref[...] = (home == iota((SLOTS, SLOTS), 1)).astype(F32).astype(BF16)


def fill_hot(key_ref, hot_ref):
    hot_ref[...] = (iota((SLOTS, SLOTS), 0) == key_ref[...]).astype(F32).astype(BF16)


def fill_select(meta, select_ref):
    cols = meta.astype(BF16)
    image = iota((GK, 1), 0) % ROWS
    owner = iota((GK, 1), 0) // ROWS
    own_ccd = jnp.where(image < CCD * BASIS, image % CCD, -1).astype(F32)
    seen = owner == iota((GK, GSLOTS), 1) // 16
    for h in range(GROUPS):
        at = slice(h * GSLOTS, (h + 1) * GSLOTS)
        hit = seen & (own_ccd == meta[QUAD * BASIS + 1 : QUAD * BASIS + 2, at])
        for q in range(QUAD):
            spread = (iota((GK, LANES), 1) == (image // CCD) * QUAD + q).astype(F32).astype(BF16)
            laid = jnp.dot(spread, cols[:, at], preferred_element_type=F32)
            select_ref[h, :, q * GSLOTS : (q + 1) * GSLOTS] = jnp.where(hit, laid, 0.0).astype(BF16)


def render(every_ref, select_ref, model_ref):
    for h in range(GROUPS):
        image = lax.dot_general(
            every_ref[h * 8 : (h + 1) * 8].reshape(GK, PADPIX),
            select_ref[h],
            (((0,), (0,)), ((), ())),
            preferred_element_type=F32,
        )
        for q in range(QUAD):
            model_ref[q, :, h * GSLOTS : (h + 1) * GSLOTS] = image[
                :, q * GSLOTS : (q + 1) * GSLOTS
            ].astype(BF16)


def accumulate(chunk, xt_ref, own_ref, model_ref, scale_ref, term_ref, rows=16):
    for lane in range(SLOTS // LANES):
        at = slice(lane * LANES, (lane + 1) * LANES)
        quarter = jnp.broadcast_to(scale_ref[0:1, at], (rows, LANES))
        live = jnp.broadcast_to(scale_ref[1:2, at], (rows, LANES))

        def step(i, sums):
            here = pl.ds(pl.multiple_of(i * rows, rows), rows)
            there = pl.ds(pl.multiple_of(chunk * LANES + i * rows, rows), rows)
            x = xt_ref[there, at].astype(F32)
            gap = x - own_ref[here, at]
            weight = live / (1.0 + quarter * (gap * gap))
            m = [model_ref[q, there, at].astype(F32) for q in range(QUAD)]
            wm = [weight * v for v in m]
            new = [wm[q] * m[r] for q, r in PAIRS] + [wm[q] * x for q in range(QUAD)]
            return tuple(s + (v[0:8] + v[8:16]) for s, v in zip(sums, new))

        sums = lax.fori_loop(
            0,
            LANES // rows,
            step,
            tuple(jnp.zeros((8, LANES), F32) for _ in range(14)),
            unroll=UNROLL,
        )
        for n, s in enumerate(sums):
            term_ref[n, :, at] += s


def finish_terms(term_ref, move_ref):
    rows = [jnp.sum(term_ref[n], axis=0, keepdims=True) for n in range(14)]
    block = jnp.concatenate(rows + [jnp.zeros((TERMS - 14, SLOTS), F32)], axis=0)
    moved = jnp.dot(
        jnp.concatenate(halves(block), axis=0), move_ref[...], preferred_element_type=F32
    )
    return moved[0:TERMS] + moved[TERMS : 2 * TERMS] + moved[2 * TERMS : 3 * TERMS]


def invert(mat_ref, zero_ref):
    lane = iota((8, LANES), 1)
    sub = iota((8, LANES), 0)
    zero = zero_ref[...]

    def spread(v, j):
        return jnp.broadcast_to(v[j : j + 1, :], (8, LANES))

    def block(i, _):
        top = pl.multiple_of(i * 8, 8)
        panel = mat_ref[pl.ds(top, 8), :]
        cols = [jnp.broadcast_to(panel[:, k : k + 1], (8, LANES)) + zero for k in range(8)]
        for j in range(8):
            factor = cols[j]
            pivot = 1.0 / spread(factor, j)
            row = jnp.where(lane == j, 1.0, spread(panel, j)) * pivot
            panel = jnp.where(sub == j, row, jnp.where(lane == j, 0.0, panel) - factor * row)
            for k in range(j + 1, 8):
                side = spread(cols[k], j) * pivot
                cols[k] = jnp.where(sub == j, side, cols[k] - factor * side)
        spreads = [spread(panel, j) for j in range(8)]
        for n in range(16):
            old = mat_ref[n * 8 : (n + 1) * 8, :]
            new = jnp.where(lane < 8, 0.0, old)
            even = zero
            for j in range(0, 8, 2):
                new = new - jnp.broadcast_to(old[:, j : j + 1], (8, LANES)) * spreads[j]
                even = even + jnp.broadcast_to(old[:, j + 1 : j + 2], (8, LANES)) * spreads[j + 1]
            new = jnp.where(n == i, panel, new - even)
            mat_ref[n * 8 : (n + 1) * 8, :] = pltpu.roll(new, LANES - 8, 1)
        return 0

    lax.fori_loop(0, 16, block, 0)


def full(a, b):
    return jnp.dot(a, b, preferred_element_type=F32, precision=HIGHEST)


def fill_home(source, home_ref):
    where = iota((ORDER, SLOTS), 0)
    for q in range(QUAD):
        home_ref[q] = (where == source[q : q + 1, :]).astype(F32).astype(BF16)


def halves(v):
    high = v.astype(BF16)
    rest = v - high.astype(F32)
    mid = rest.astype(BF16)
    return high, mid, (rest - mid.astype(F32)).astype(BF16)


def solve(terms, home_ref, side_ref, work_ref, zero_ref):
    gram = jnp.zeros((ORDER, ORDER), F32)
    row = jnp.zeros((8, ORDER), F32)
    for r in range(QUAD):
        for part in range(2):
            mixed = None
            for q in range(r + 1):
                value = terms[PAIRS.index((q, r)) : PAIRS.index((q, r)) + 1, :]
                value = halves(value * (0.5 if q == r else 1.0))[part]
                step = home_ref[q] * value
                mixed = step if mixed is None else mixed + step
            side_ref[part * ORDER : (part + 1) * ORDER, :] = mixed
        one, two, three = halves(terms[10 + r : 11 + r, :])
        side_ref[2 * ORDER : 2 * ORDER + 16, :] = jnp.concatenate(
            [one.astype(F32), two.astype(F32), three.astype(F32), jnp.zeros((13, SLOTS), F32)], axis=0
        ).astype(BF16)
        got = lax.dot_general(
            side_ref[...], home_ref[r], (((1,), (1,)), ((), ())), preferred_element_type=F32
        )
        gram = gram + (got[:ORDER] + got[ORDER : 2 * ORDER])
        row = row + got[2 * ORDER : 2 * ORDER + 8]
    row = row[0:1] + row[1:2] + row[2:3]
    eye = iota((HALF, HALF), 0) == iota((HALF, HALF), 1)
    one = jnp.where(eye, 1.0, 0.0)

    def turn(v):
        return jnp.transpose(jnp.broadcast_to(v, (HALF, HALF)))

    a11 = gram[:HALF, :HALF]
    a22 = gram[HALF:, HALF:]
    a12 = gram[:HALF, HALF:] + jnp.transpose(gram[HALF:, :HALF])
    a21 = jnp.transpose(a12)
    r1_row, r2_row = row[:, :HALF], row[:, HALF:]
    r1_col, r2_col = turn(r1_row)[:, 0:1], turn(r2_row)[:, 0:1]
    work_ref[...] = a11 + jnp.transpose(a11) + one
    invert(work_ref, zero_ref)
    top = work_ref[...]
    tie = full(a21, top)
    work_ref[...] = a22 + jnp.transpose(a22) + one - full(tie, a12)
    invert(work_ref, zero_ref)
    low = work_ref[...]
    v = r2_col - jnp.sum(tie * r1_row, axis=1, keepdims=True)
    f2_row = jnp.sum(low * v, axis=0, keepdims=True)
    f2_col = jnp.sum(low * turn(v)[0:1, :], axis=1, keepdims=True)
    f1_row = jnp.sum(top * r1_col, axis=0, keepdims=True) - jnp.sum(tie * f2_col, axis=0, keepdims=True)
    d2 = jnp.sum(jnp.where(eye, low, 0.0), axis=0, keepdims=True)
    d1 = jnp.sum(jnp.where(eye, top, 0.0), axis=0, keepdims=True) + jnp.sum(
        full(low, tie) * tie, axis=0, keepdims=True
    )
    return f1_row / jnp.sqrt(d1), f2_row / jnp.sqrt(d2)


def remote(src, dst, send, recv, **where):
    return pltpu.make_async_remote_copy(
        src_ref=src, dst_ref=dst, send_sem=send, recv_sem=recv, device_id=where, device_id_type=MESH
    )


def whole_kernel(
    st_ref, cf_ref, iv_ref, cd_ref, src_ref, counts_ref, bases_ref, out_ref,
    mine_ref, key_ref, move_ref, meta_out, meta_in, src_out, src_in, home_ref, side_ref, zero_ref,
    packed, got, every, xt_ref, hot_ref, select_ref, model_ref, scale_ref, own_ref, term_ref,
    tables, parts, mean_own, means, count_ref, terms_out, terms_in, work_ref,
    a_send, a_recv, b_send, b_recv, t_send, t_recv, m_send, m_recv, e_send, e_recv, s_send, s_recv,
):
    me = lax.axis_index("tile")
    g = lax.axis_index("rep")
    x, z, c = me // 16, (me // 2) % 8, me % 2

    def peer(dx, dz, core):
        return (((x + dx + 4) % 4) * 8 + (z + dz + 8) % 8) * 2 + core

    barrier = pltpu.get_barrier_semaphore()

    def greet(o, _):
        pl.semaphore_signal(barrier, inc=1, device_id={"tile": (me + o) % TILES}, device_id_type=MESH)
        return 0

    lax.fori_loop(1, TILES, greet, 0)
    for d in range(1, REPS):
        pl.semaphore_signal(barrier, inc=1, device_id={"rep": (g + d) % REPS}, device_id_type=MESH)

    def send_all(src, dst, n):
        def one(o, _):
            p = (me + o) % TILES
            remote(src.at[p], dst.at[me], a_send.at[n], a_recv.at[n], tile=p).start()
            return 0

        lax.fori_loop(1, TILES, one, 0)
        dst[pl.ds(me, 1)] = src[pl.ds(me, 1)]

    def all_done(src, dst, n):
        many = pl.ds(0, TILES - 1)
        return remote(src.at[many], dst.at[many], a_send.at[n], a_recv.at[n], tile=peer(0, 1, c))

    def send_block(n):
        send_all(packed.at[n], got.at[n], n)

    def block_done(n):
        return all_done(packed.at[n], got.at[n], n)

    def blocks_done(stage, count):
        many = every.at[pl.ds(0, count), 0]
        return remote(many, many, b_send.at[stage], b_recv.at[stage], tile=peer(0, 1, c))

    def send_bases(stage, ref, dx, dz, core):
        remote(ref, ref, b_send.at[stage], b_recv.at[stage], tile=peer(dx, dz, core)).start()

    here = x * 8 + z

    def stage_z1():
        for dz in (1, -1, 2, -2):
            remote(
                mine_ref, every.at[here, c], b_send.at[0], b_recv.at[0], tile=peer(0, dz, c)
            ).start()

    def stage_z2():
        blocks_done(0, 4).wait_recv()
        low = every.at[x * 8 + (z + 6) % 8, c]
        high = every.at[x * 8 + (z + 2) % 8, c]
        send_bases(1, low, 0, 1, c)
        send_bases(1, high, 0, -1, c)
        send_bases(1, low, 0, 2, c)

    def stage_x1():
        blocks_done(1, 3).wait_recv()
        mid = every.at[pl.ds(x * 8, 8), c]
        send_bases(2, mid, 1, 0, c)
        send_bases(2, mid, -1, 0, c)

    def stage_x2():
        blocks_done(2, 16).wait_recv()
        send_bases(3, every.at[pl.ds(((x + 3) % 4) * 8, 4), c], 1, 0, c)
        send_bases(3, every.at[pl.ds(((x + 1) % 4) * 8 + 4, 4), c], -1, 0, c)

    def column(shift):
        return pl.ds(((x + shift) % 4) * 8, 8)

    def stage_core1():
        send_bases(4, every.at[column(0), c], 0, 0, 1 - c)

    def stage_core2():
        send_bases(5, every.at[column(1), c], 0, 0, 1 - c)
        send_bases(5, every.at[column(3), c], 0, 0, 1 - c)

    def stage_core3():
        blocks_done(3, 8).wait_recv()
        send_bases(6, every.at[column(2), c], 0, 0, 1 - c)

    def stack(n):
        block_done(n).wait_recv()
        turned = jnp.transpose(got[n].reshape(SLOTS, LANES).astype(F32)).astype(BF16)
        xt_ref[n * LANES : (n + 1) * LANES, :] = turned
        part = lax.dot_general(
            turned, hot_ref[...], (((1,), (1,)), ((), ())), preferred_element_type=F32
        )
        for b in range(REPS):
            tables[n, b] = part[:, b * ORDER : (b + 1) * ORDER].astype(BF16)
        for d in range(1, REPS):
            b = (g + d) % REPS
            remote(tables.at[n, b], parts.at[n, g], t_send.at[n], t_recv.at[n], rep=b).start()
        parts[n, pl.ds(g, 1)] = tables[n, pl.ds(g, 1)]

    def three(src, dst, send, recv, n):
        many = pl.ds(0, REPS - 1)
        return remote(src.at[n, many], dst.at[n, many], send.at[n], recv.at[n], rep=(g + 1) % REPS)

    def mean(n):
        three(tables, parts, t_send, t_recv, n).wait_recv()
        total = parts[n, 0].astype(F32)
        for other in range(1, REPS):
            total = total + parts[n, other].astype(F32)
        if n == CHUNKS - 1:
            at = PIX - (CHUNKS - 1) * LANES
            count_ref[...] = jnp.broadcast_to(total[at : at + 1, :], (8, ORDER))
        value = (total / (1.0 + count_ref[0:1, :])).astype(BF16)
        mean_own[n, 0] = value
        for d in range(1, REPS):
            remote(
                mean_own.at[n, 0], means.at[n, g], m_send.at[n], m_recv.at[n], rep=(g + d) % REPS
            ).start()
        means[n, pl.ds(g, 1)] = mean_own[n]

    def terms(n):
        three(means, means, m_send, m_recv, n).wait_recv()
        joined = jnp.concatenate([means[n, b] for b in range(REPS)], axis=1)
        own_ref[...] = jnp.dot(joined, hot_ref[...], preferred_element_type=F32)
        accumulate(n, xt_ref, own_ref, model_ref, scale_ref, term_ref)

    pack_meta(cf_ref, iv_ref, cd_ref, meta_out)
    pack_block(st_ref, 4, packed)
    mine_ref[...] = jnp.zeros_like(mine_ref)
    mine_ref[0 : CCD * BASIS, 0:PIX] = jnp.concatenate(
        [bases_ref[k].astype(F32) for k in range(BASIS)], axis=0
    ).astype(BF16)
    pl.semaphore_wait(barrier, TILES - 1 + REPS - 1)
    stage_z1()
    send_all(meta_out, meta_in, CHUNKS)
    send_block(4)
    every[pl.ds(here, 1), pl.ds(c, 1)] = mine_ref[...].reshape(1, 1, ROWS, PADPIX)
    pack_block(st_ref, 0, packed)
    stage_z2()
    send_block(0)
    pack_block(st_ref, 1, packed)
    stage_x1()
    stage_core1()
    send_block(1)
    pack_block(st_ref, 2, packed)
    pack_block(st_ref, 3, packed)
    send_block(2)
    fill_key(counts_ref, src_ref, key_ref)
    fill_hot(key_ref, hot_ref)
    fill_move(move_ref)
    wide = jnp.concatenate([src_ref[...].astype(F32), jnp.zeros((12, SLOTS), F32)], axis=0)
    wide = jnp.dot(wide.astype(BF16), move_ref[...], preferred_element_type=F32)
    for b in range(REPS):
        src_out[0, b] = wide[0:8, b * ORDER : (b + 1) * ORDER]
    for d in range(1, REPS):
        b = (g + d) % REPS
        remote(src_out.at[0, b], src_in.at[0, g], s_send.at[0], s_recv.at[0], rep=b).start()
    src_in[0, pl.ds(g, 1)] = src_out[0, pl.ds(g, 1)]
    stage_x2()
    stage_core2()
    send_block(3)
    term_ref[...] = jnp.zeros_like(term_ref)
    zero_ref[...] = jnp.zeros_like(zero_ref)
    all_done(meta_out, meta_in, CHUNKS).wait_recv()
    meta = unpack_meta(meta_in)
    ivar = meta[QUAD * BASIS : QUAD * BASIS + 1, :]
    scale_ref[0:1, :] = ivar * 0.25
    scale_ref[1:2, :] = jnp.where(key_ref[...] >= 0, ivar, 0.0)
    fill_select(meta, select_ref)
    stack(4)
    stage_core3()
    stack(0)
    mean(4)
    three(src_out, src_in, s_send, s_recv, 0).wait_recv()
    fill_home(
        jnp.concatenate([src_in[0, k] for k in range(REPS)], axis=1).astype(I32), home_ref
    )
    stack(1)
    mean(0)
    stack(2)
    mean(1)
    blocks_done(4, 8).wait_recv()
    blocks_done(5, 16).wait_recv()
    blocks_done(6, 8).wait_recv()
    render(every, select_ref, model_ref)
    terms(4)
    stack(3)
    mean(2)
    terms(0)
    terms(1)
    mean(3)
    terms(2)
    terms(3)
    block = finish_terms(term_ref, move_ref)
    for b in range(REPS):
        terms_out[0, b] = block[:, b * ORDER : (b + 1) * ORDER]
    for d in range(1, REPS):
        b = (g + d) % REPS
        remote(terms_out.at[0, b], terms_in.at[0, g], e_send.at[0], e_recv.at[0], rep=b).start()
    terms_in[0, pl.ds(g, 1)] = terms_out[0, pl.ds(g, 1)]
    three(terms_out, terms_in, e_send, e_recv, 0).wait_recv()
    joined = jnp.concatenate([terms_in[0, k] for k in range(REPS)], axis=1)
    left, right = solve(joined, home_ref, side_ref, work_ref, zero_ref)
    out_ref[:, :HALF] = left
    out_ref[:, HALF:] = right

    for n in range(CHUNKS):
        block_done(n).wait_send()
    all_done(meta_out, meta_in, CHUNKS).wait_send()
    three(src_out, src_in, s_send, s_recv, 0).wait_send()
    for stage, count in enumerate((4, 3, 16, 8, 8, 16, 8)):
        blocks_done(stage, count).wait_send()
    for n in range(CHUNKS):
        three(tables, parts, t_send, t_recv, n).wait_send()
        three(means, means, m_send, m_recv, n).wait_send()
    three(terms_out, terms_in, e_send, e_recv, 0).wait_send()


def struct(shape, dtype):
    return jax.ShapeDtypeStruct(shape, dtype)


def local(stamps, coefs, ivar, ccd, bases, sources, counts):
    dma = pltpu.SemaphoreType.DMA
    return pl.pallas_call(
        whole_kernel,
        out_shape=struct((1, ORDER), F32),
        in_specs=[VMEM] * 7,
        out_specs=VMEM,
        scratch_shapes=[
            pltpu.VMEM((ROWS, PADPIX), BF16),
            pltpu.VMEM((1, SLOTS), I32),
            pltpu.VMEM((SLOTS, SLOTS), BF16),
            pltpu.VMEM((TILES, 8, LANES), BF16),
            pltpu.VMEM((TILES, 8, LANES), BF16),
            pltpu.VMEM((1, REPS, 8, ORDER), F32),
            pltpu.VMEM((1, REPS, 8, ORDER), F32),
            pltpu.VMEM((QUAD, ORDER, SLOTS), BF16),
            pltpu.VMEM((2 * ORDER + 16, SLOTS), BF16),
            pltpu.VMEM((8, LANES), F32),
            pltpu.VMEM((CHUNKS, TILES, 16, LANES), BF16),
            pltpu.VMEM((CHUNKS, TILES, 16, LANES), BF16),
            pltpu.VMEM((32, 2, ROWS, PADPIX), BF16),
            pltpu.VMEM((PADPIX, SLOTS), BF16),
            pltpu.VMEM((SLOTS, SLOTS), BF16),
            pltpu.VMEM((GROUPS, GK, QUAD * GSLOTS), BF16),
            pltpu.VMEM((QUAD, PADPIX, SLOTS), BF16),
            pltpu.VMEM((8, SLOTS), F32),
            pltpu.VMEM((LANES, SLOTS), F32),
            pltpu.VMEM((14, 8, SLOTS), F32),
            pltpu.VMEM((CHUNKS, REPS, LANES, ORDER), BF16),
            pltpu.VMEM((CHUNKS, REPS, LANES, ORDER), BF16),
            pltpu.VMEM((CHUNKS, 1, LANES, ORDER), BF16),
            pltpu.VMEM((CHUNKS, REPS, LANES, ORDER), BF16),
            pltpu.VMEM((8, ORDER), F32),
            pltpu.VMEM((1, REPS, TERMS, ORDER), F32),
            pltpu.VMEM((1, REPS, TERMS, ORDER), F32),
            pltpu.VMEM((HALF, HALF), F32),
            dma((CHUNKS + 1,)),
            dma((CHUNKS + 1,)),
            dma((7,)),
            dma((7,)),
            dma((CHUNKS,)),
            dma((CHUNKS,)),
            dma((CHUNKS,)),
            dma((CHUNKS,)),
            dma((1,)),
            dma((1,)),
            dma((1,)),
            dma((1,)),
        ],
        compiler_params=pltpu.CompilerParams(
            collective_id=0, has_side_effects=True, vmem_limit_bytes=60 * 1024 * 1024
        ),
    )(
        stamps,
        jnp.transpose(coefs, (1, 0, 2)),
        ivar.reshape(8, LANES),
        ccd.reshape(8, LANES),
        sources,
        jnp.transpose(counts),
        jnp.transpose(bases, (1, 0, 2)),
    )


def solution(mesh):
    return jax.shard_map(
        local,
        mesh=mesh,
        in_specs=(
            P(None, ("tile", "rep")),
            P(None, None, ("tile", "rep")),
            P(("tile", "rep")),
            P(("tile", "rep")),
            P(("tile", "rep"), None, None),
            P(None, ("tile", "rep")),
            P(("tile", "rep"), None),
        ),
        out_specs=P(("tile", "rep"), None),
        check_vma=False,
    )
```

time: 146 us -> 112 us (0.77)
  Pallas kernels: 137 us -> 110 us
  local copies, waits for them, and re-layouts: 6.44 us -> 1.24 us
  other arithmetic: 1.46 us -> 0 us
    pallas_call x1, Pallas kernels: 137 us -> 110 us  [local(): pl.pallas_call(whole_kernel, out_shape=struct((1, ORDER), F32), in_specs=...]
    unnamed x4 -> x1, local copies, waits for them, and re-layouts: 3.7 us -> 1.24 us
    reshape x3 -> x0, local copies, waits for them, and re-layouts: 1.97 us -> none  [the longest x1 1.28 us: local(): ivar.reshape(1, SLOTS)]
where the time goes in v2:
time: 112 us; the launch traced here: 111 us
  Pallas kernels  110 us (98%)
  local copies, waits for them, and re-layouts  1.24 us (1%)
    pallas_call x1, Pallas kernels, local(): pl.pallas_call(whole_kernel, out_shape=struct((1, ORDER), F32), in_specs=...  110 us

profile of v2, /device:TPU:2, one launch (start us, length us, event | category | flops | bytes accessed | tf_op | source)
XLA Modules:
  0.0 111.3 jit_solution(217196365401084385)
XLA Ops:
  0.0 110.1 %shard_map.73 = f32[1,256]{1,0:T(1,128)} custom-call(bf16[625,1024]{1,0:T(8,128)(2,1)} %st_ref.1, bf16[10,4,1024]{2,1,0:T(4,128)(2,1)} %bitcast.5, bf16[8,128]{1,0:T(8,128)(2,1)} %bitcast.8, s32[8,128]{1,0:T(8,128)} %bitcast.7, s32[4,1024]{1,0:T(4,128)} %src_ref.1, s32[4,64]{1,0:T(4,128)} %bitcast.9, bf16[10,4,625]{2,1,0:T(4,128)(2,1)} %bitcast.6), custom_call_target="tpu_custom_call" | custom-call | tf_op jit(solution)/shard_map/pallas_call | solution.py:507
  110.1 1.2 %copy.9 = f32[1,256]{1,0:T(1,128)} copy(f32[1,256]{1,0:T(1,128)} %shard_map.73) | data formatting | bytes 2048

commit v3 on v2

--- a/solution.py
+++ b/solution.py
@@ -101,31 +101,37 @@
 
 def fill_select(meta, select_ref):
     cols = meta.astype(BF16)
-    image = iota((GK, 1), 0) % ROWS
-    owner = iota((GK, 1), 0) // ROWS
+    image = iota((ROWS, 1), 0)
     own_ccd = jnp.where(image < CCD * BASIS, image % CCD, -1).astype(F32)
-    seen = owner == iota((GK, GSLOTS), 1) // 16
-    for h in range(GROUPS):
-        at = slice(h * GSLOTS, (h + 1) * GSLOTS)
-        hit = seen & (own_ccd == meta[QUAD * BASIS + 1 : QUAD * BASIS + 2, at])
-        for q in range(QUAD):
-            spread = (iota((GK, LANES), 1) == (image // CCD) * QUAD + q).astype(F32).astype(BF16)
-            laid = jnp.dot(spread, cols[:, at], preferred_element_type=F32)
-            select_ref[h, :, q * GSLOTS : (q + 1) * GSLOTS] = jnp.where(hit, laid, 0.0).astype(BF16)
-
-
-def render(every_ref, select_ref, model_ref):
-    for h in range(GROUPS):
-        image = lax.dot_general(
-            every_ref[h * 8 : (h + 1) * 8].reshape(GK, PADPIX),
-            select_ref[h],
-            (((0,), (0,)), ((), ())),
-            preferred_element_type=F32,
-        )
-        for q in range(QUAD):
-            model_ref[q, :, h * GSLOTS : (h + 1) * GSLOTS] = image[
-                :, q * GSLOTS : (q + 1) * GSLOTS
-            ].astype(BF16)
+    hit = own_ccd == meta[QUAD * BASIS + 1 : QUAD * BASIS + 2, :]
+    owner = iota((16, GSLOTS), 1) // 16
+    laid = []
+    for q in range(QUAD):
+        spread = (iota((ROWS, LANES), 1) == (image // CCD) * QUAD + q).astype(F32).astype(BF16)
+        value = jnp.dot(spread, cols, preferred_element_type=F32)
+        laid.append(jnp.where(hit, value, 0.0).astype(BF16))
+    for t in range(GROUP):
+        seen = (owner == t).astype(F32).astype(BF16)
+        for h in range(GROUPS):
+            for q in range(QUAD):
+                for part in range(ROWS // 16):
+                    select_ref[
+                        h,
+                        t * ROWS + part * 16 : t * ROWS + (part + 1) * 16,
+                        q * GSLOTS : (q + 1) * GSLOTS,
+                    ] = seen * laid[q][part * 16 : (part + 1) * 16, h * GSLOTS : (h + 1) * GSLOTS]
+
+
+def render(h, every_ref, select_ref, model_ref):
+    image = lax.dot_general(
+        every_ref[pl.ds(h * 8, 8)].reshape(GK, PADPIX),
+        select_ref[h],
+        (((0,), (0,)), ((), ())),
+        preferred_element_type=F32,
+    )
+    at = pl.ds(pl.multiple_of(h * GSLOTS, GSLOTS), GSLOTS)
+    for q in range(QUAD):
+        model_ref[q, :, at] = image[:, q * GSLOTS : (q + 1) * GSLOTS].astype(BF16)
 
 
 def accumulate(chunk, xt_ref, own_ref, model_ref, scale_ref, term_ref, rows=16):
@@ -173,31 +179,47 @@
     def spread(v, j):
         return jnp.broadcast_to(v[j : j + 1, :], (8, LANES))
 
-    def block(i, _):
-        top = pl.multiple_of(i * 8, 8)
-        panel = mat_ref[pl.ds(top, 8), :]
-        cols = [jnp.broadcast_to(panel[:, k : k + 1], (8, LANES)) + zero for k in range(8)]
-        for j in range(8):
-            factor = cols[j]
-            pivot = 1.0 / spread(factor, j)
-            row = jnp.where(lane == j, 1.0, spread(panel, j)) * pivot
-            panel = jnp.where(sub == j, row, jnp.where(lane == j, 0.0, panel) - factor * row)
-            for k in range(j + 1, 8):
-                side = spread(cols[k], j) * pivot
-                cols[k] = jnp.where(sub == j, side, cols[k] - factor * side)
-        spreads = [spread(panel, j) for j in range(8)]
-        for n in range(16):
-            old = mat_ref[n * 8 : (n + 1) * 8, :]
-            new = jnp.where(lane < 8, 0.0, old)
-            even = zero
-            for j in range(0, 8, 2):
-                new = new - jnp.broadcast_to(old[:, j : j + 1], (8, LANES)) * spreads[j]
-                even = even + jnp.broadcast_to(old[:, j + 1 : j + 2], (8, LANES)) * spreads[j + 1]
-            new = jnp.where(n == i, panel, new - even)
-            mat_ref[n * 8 : (n + 1) * 8, :] = pltpu.roll(new, LANES - 8, 1)
+    def block(o, _):
+        top = pl.multiple_of(o * 32, 32)
+        rows = [mat_ref[pl.ds(top + 8 * m, 8), :] for m in range(4)]
+        for kb in range(4):
+            base = 8 * kb
+            panel = rows[kb]
+            cols = [
+                jnp.broadcast_to(panel[:, base + k : base + k + 1], (8, LANES)) + zero
+                for k in range(8)
+            ]
+            for j in range(8):
+                factor = cols[j]
+                pivot = 1.0 / spread(factor, j)
+                row = jnp.where(lane == base + j, 1.0, spread(panel, j)) * pivot
+                kept = jnp.where(lane == base + j, 0.0, panel)
+                panel = jnp.where(sub == j, row, kept - factor * row)
+                for k in range(j + 1, 8):
+                    side = spread(cols[k], j) * pivot
+                    cols[k] = jnp.where(sub == j, side, cols[k] - factor * side)
+            spreads = [spread(panel, j) for j in range(8)]
+            rows[kb] = panel
+            for m in range(4):
+                if m == kb:
+                    continue
+                old = rows[m]
+                new = jnp.where((lane >= base) & (lane < base + 8), 0.0, old)
+                even = zero
+                for j in range(0, 8, 2):
+                    a = jnp.broadcast_to(old[:, base + j : base + j + 1], (8, LANES))
+                    b = jnp.broadcast_to(old[:, base + j + 1 : base + j + 2], (8, LANES))
+                    new = new - a * spreads[j]
+                    even = even + b * spreads[j + 1]
+                rows[m] = new - even
+        whole = mat_ref[...]
+        done = jnp.concatenate(rows, axis=0)
+        kept = jnp.where(iota((HALF, LANES), 1) < 32, 0.0, whole)
+        mat_ref[...] = pltpu.roll(kept - full(whole[:, 0:32], done), LANES - 32, 1)
+        mat_ref[pl.ds(top, 32), :] = pltpu.roll(done, LANES - 32, 1)
         return 0
 
-    lax.fori_loop(0, 16, block, 0)
+    lax.fori_loop(0, 4, block, 0)
 
 
 def full(a, b):
@@ -327,6 +349,9 @@
 
     here = x * 8 + z
 
+    def origin(dx, dz):
+        return every.at[((x + dx + 4) % 4) * 8 + (z + dz + 8) % 8, c]
+
     def stage_z1():
         for dz in (1, -1, 2, -2):
             remote(
@@ -334,23 +359,20 @@
             ).start()
 
     def stage_z2():
-        blocks_done(0, 4).wait_recv()
-        low = every.at[x * 8 + (z + 6) % 8, c]
-        high = every.at[x * 8 + (z + 2) % 8, c]
-        send_bases(1, low, 0, 1, c)
-        send_bases(1, high, 0, -1, c)
-        send_bases(1, low, 0, 2, c)
-
-    def stage_x1():
-        blocks_done(1, 3).wait_recv()
-        mid = every.at[pl.ds(x * 8, 8), c]
-        send_bases(2, mid, 1, 0, c)
-        send_bases(2, mid, -1, 0, c)
-
-    def stage_x2():
-        blocks_done(2, 16).wait_recv()
-        send_bases(3, every.at[pl.ds(((x + 3) % 4) * 8, 4), c], 1, 0, c)
-        send_bases(3, every.at[pl.ds(((x + 1) % 4) * 8 + 4, 4), c], -1, 0, c)
+        send_bases(1, origin(0, -2), 0, 1, c)
+        send_bases(1, origin(0, 2), 0, -1, c)
+        send_bases(1, origin(0, -2), 0, 2, c)
+
+    def stage_x1(stage, offsets):
+        for dz in offsets:
+            for dx in (1, -1):
+                send_bases(stage, origin(0, dz), dx, 0, c)
+
+    def stage_x2(stage, ahead, back):
+        for dz in ahead:
+            send_bases(stage, origin(-1, dz), 1, 0, c)
+        for dz in back:
+            send_bases(stage, origin(1, dz), -1, 0, c)
 
     def column(shift):
         return pl.ds(((x + shift) % 4) * 8, 8)
@@ -363,8 +385,12 @@
         send_bases(5, every.at[column(3), c], 0, 0, 1 - c)
 
     def stage_core3():
-        blocks_done(3, 8).wait_recv()
+        blocks_done(3, 5).wait_recv()
+        blocks_done(8, 3).wait_recv()
         send_bases(6, every.at[column(2), c], 0, 0, 1 - c)
+
+    def show(shift):
+        render((x + shift) % 4, every, select_ref, model_ref)
 
     def stack(n):
         block_done(n).wait_recv()
@@ -414,19 +440,28 @@
     ).astype(BF16)
     pl.semaphore_wait(barrier, TILES - 1 + REPS - 1)
     stage_z1()
+    every[pl.ds(here, 1), pl.ds(c, 1)] = mine_ref[...].reshape(1, 1, ROWS, PADPIX)
+    pack_block(st_ref, 0, packed)
+    blocks_done(0, 4).wait_recv()
+    stage_z2()
+    stage_x1(2, (0, 1, -1, 2, -2))
     send_all(meta_out, meta_in, CHUNKS)
     send_block(4)
-    every[pl.ds(here, 1), pl.ds(c, 1)] = mine_ref[...].reshape(1, 1, ROWS, PADPIX)
-    pack_block(st_ref, 0, packed)
-    stage_z2()
+    pack_block(st_ref, 1, packed)
+    blocks_done(1, 3).wait_recv()
+    stage_x1(7, (3, 4, -3))
+    stage_core1()
     send_block(0)
-    pack_block(st_ref, 1, packed)
-    stage_x1()
-    stage_core1()
     send_block(1)
     pack_block(st_ref, 2, packed)
     pack_block(st_ref, 3, packed)
+    blocks_done(2, 10).wait_recv()
+    stage_x2(3, (0, 1, 2), (-1, -2))
+    blocks_done(7, 6).wait_recv()
+    stage_x2(8, (3, 4), (-3,))
+    stage_core2()
     send_block(2)
+    send_block(3)
     fill_key(counts_ref, src_ref, key_ref)
     fill_hot(key_ref, hot_ref)
     fill_move(move_ref)
@@ -438,9 +473,6 @@
         b = (g + d) % REPS
         remote(src_out.at[0, b], src_in.at[0, g], s_send.at[0], s_recv.at[0], rep=b).start()
     src_in[0, pl.ds(g, 1)] = src_out[0, pl.ds(g, 1)]
-    stage_x2()
-    stage_core2()
-    send_block(3)
     term_ref[...] = jnp.zeros_like(term_ref)
     zero_ref[...] = jnp.zeros_like(zero_ref)
     all_done(meta_out, meta_in, CHUNKS).wait_recv()
@@ -449,22 +481,25 @@
     scale_ref[0:1, :] = ivar * 0.25
     scale_ref[1:2, :] = jnp.where(key_ref[...] >= 0, ivar, 0.0)
     fill_select(meta, select_ref)
+    blocks_done(4, 8).wait_recv()
+    show(0)
     stack(4)
-    stage_core3()
-    stack(0)
-    mean(4)
     three(src_out, src_in, s_send, s_recv, 0).wait_recv()
     fill_home(
         jnp.concatenate([src_in[0, k] for k in range(REPS)], axis=1).astype(I32), home_ref
     )
+    stack(0)
+    mean(4)
+    blocks_done(5, 16).wait_recv()
+    show(1)
+    show(3)
     stack(1)
     mean(0)
+    stage_core3()
     stack(2)
     mean(1)
-    blocks_done(4, 8).wait_recv()
-    blocks_done(5, 16).wait_recv()
     blocks_done(6, 8).wait_recv()
-    render(every, select_ref, model_ref)
+    show(2)
     terms(4)
     stack(3)
     mean(2)
@@ -490,7 +525,7 @@
         block_done(n).wait_send()
     all_done(meta_out, meta_in, CHUNKS).wait_send()
     three(src_out, src_in, s_send, s_recv, 0).wait_send()
-    for stage, count in enumerate((4, 3, 16, 8, 8, 16, 8)):
+    for stage, count in enumerate((4, 3, 10, 5, 8, 16, 8, 6, 3)):
         blocks_done(stage, count).wait_send()
     for n in range(CHUNKS):
         three(tables, parts, t_send, t_recv, n).wait_send()
@@ -540,8 +575,8 @@
             pltpu.VMEM((HALF, HALF), F32),
             dma((CHUNKS + 1,)),
             dma((CHUNKS + 1,)),
-            dma((7,)),
-            dma((7,)),
+            dma((9,)),
+            dma((9,)),
             dma((CHUNKS,)),
             dma((CHUNKS,)),
             dma((CHUNKS,)),

time: 112 us -> 97.2 us (0.87)
  Pallas kernels: 110 us -> 95.5 us
    pallas_call x1, Pallas kernels: 110 us -> 95.5 us  [local(): pl.pallas_call(whole_kernel, out_shape=struct((1, ORDER), F32), in_specs=...]
where the time goes in v3:
time: 97.2 us; the launch traced here: 96.8 us
  Pallas kernels  95.5 us (98%)
  local copies, waits for them, and re-layouts  1.24 us (1%)
    pallas_call x1, Pallas kernels, local(): pl.pallas_call(whole_kernel, out_shape=struct((1, ORDER), F32), in_specs=...  95.5 us

profile of v3, /device:TPU:2, one launch (start us, length us, event | category | flops | bytes accessed | tf_op | source)
XLA Modules:
  0.0 96.8 jit_solution(1317790097302259544)
XLA Ops:
  0.0 95.5 %shard_map.73 = f32[1,256]{1,0:T(1,128)} custom-call(bf16[625,1024]{1,0:T(8,128)(2,1)} %st_ref.1, bf16[10,4,1024]{2,1,0:T(4,128)(2,1)} %bitcast.5, bf16[8,128]{1,0:T(8,128)(2,1)} %bitcast.8, s32[8,128]{1,0:T(8,128)} %bitcast.7, s32[4,1024]{1,0:T(4,128)} %src_ref.1, s32[4,64]{1,0:T(4,128)} %bitcast.9, bf16[10,4,625]{2,1,0:T(4,128)(2,1)} %bitcast.6), custom_call_target="tpu_custom_call" | custom-call | tf_op jit(solution)/shard_map/pallas_call | solution.py:542
  95.5 1.2 %copy.9 = f32[1,256]{1,0:T(1,128)} copy(f32[1,256]{1,0:T(1,128)} %shard_map.73) | data formatting | bytes 2048

commit v4 on v3

--- a/solution.py
+++ b/solution.py
@@ -442,28 +442,14 @@
     stage_z1()
     every[pl.ds(here, 1), pl.ds(c, 1)] = mine_ref[...].reshape(1, 1, ROWS, PADPIX)
     pack_block(st_ref, 0, packed)
+    fill_key(counts_ref, src_ref, key_ref)
+    fill_hot(key_ref, hot_ref)
     blocks_done(0, 4).wait_recv()
     stage_z2()
     stage_x1(2, (0, 1, -1, 2, -2))
     send_all(meta_out, meta_in, CHUNKS)
     send_block(4)
     pack_block(st_ref, 1, packed)
-    blocks_done(1, 3).wait_recv()
-    stage_x1(7, (3, 4, -3))
-    stage_core1()
-    send_block(0)
-    send_block(1)
-    pack_block(st_ref, 2, packed)
-    pack_block(st_ref, 3, packed)
-    blocks_done(2, 10).wait_recv()
-    stage_x2(3, (0, 1, 2), (-1, -2))
-    blocks_done(7, 6).wait_recv()
-    stage_x2(8, (3, 4), (-3,))
-    stage_core2()
-    send_block(2)
-    send_block(3)
-    fill_key(counts_ref, src_ref, key_ref)
-    fill_hot(key_ref, hot_ref)
     fill_move(move_ref)
     wide = jnp.concatenate([src_ref[...].astype(F32), jnp.zeros((12, SLOTS), F32)], axis=0)
     wide = jnp.dot(wide.astype(BF16), move_ref[...], preferred_element_type=F32)
@@ -473,6 +459,13 @@
         b = (g + d) % REPS
         remote(src_out.at[0, b], src_in.at[0, g], s_send.at[0], s_recv.at[0], rep=b).start()
     src_in[0, pl.ds(g, 1)] = src_out[0, pl.ds(g, 1)]
+    blocks_done(1, 3).wait_recv()
+    stage_x1(7, (3, 4, -3))
+    stage_core1()
+    send_block(0)
+    pack_block(st_ref, 2, packed)
+    pack_block(st_ref, 3, packed)
+    send_block(1)
     term_ref[...] = jnp.zeros_like(term_ref)
     zero_ref[...] = jnp.zeros_like(zero_ref)
     all_done(meta_out, meta_in, CHUNKS).wait_recv()
@@ -481,13 +474,20 @@
     scale_ref[0:1, :] = ivar * 0.25
     scale_ref[1:2, :] = jnp.where(key_ref[...] >= 0, ivar, 0.0)
     fill_select(meta, select_ref)
+    blocks_done(2, 10).wait_recv()
+    stage_x2(3, (0, 1, 2), (-1, -2))
+    blocks_done(7, 6).wait_recv()
+    stage_x2(8, (3, 4), (-3,))
+    stage_core2()
+    send_block(2)
+    send_block(3)
+    three(src_out, src_in, s_send, s_recv, 0).wait_recv()
+    fill_home(
+        jnp.concatenate([src_in[0, k] for k in range(REPS)], axis=1).astype(I32), home_ref
+    )
     blocks_done(4, 8).wait_recv()
     show(0)
     stack(4)
-    three(src_out, src_in, s_send, s_recv, 0).wait_recv()
-    fill_home(
-        jnp.concatenate([src_in[0, k] for k in range(REPS)], axis=1).astype(I32), home_ref
-    )
     stack(0)
     mean(4)
     blocks_done(5, 16).wait_recv()

time: 97.2 us -> 94.8 us (0.975)
  Pallas kernels: 95.5 us -> 93.5 us
    pallas_call x1, Pallas kernels: 95.5 us -> 93.5 us  [local(): pl.pallas_call(whole_kernel, out_shape=struct((1, ORDER), F32), in_specs=...]
where the time goes in v4:
time: 94.8 us; the launch traced here: 94.7 us
  Pallas kernels  93.5 us (99%)
  local copies, waits for them, and re-layouts  1.24 us (1%)
    pallas_call x1, Pallas kernels, local(): pl.pallas_call(whole_kernel, out_shape=struct((1, ORDER), F32), in_specs=...  93.5 us

profile of v4, /device:TPU:2, one launch (start us, length us, event | category | flops | bytes accessed | tf_op | source)
XLA Modules:
  0.0 94.7 jit_solution(17093670174645840532)
XLA Ops:
  0.0 93.5 %shard_map.73 = f32[1,256]{1,0:T(1,128)} custom-call(bf16[625,1024]{1,0:T(8,128)(2,1)} %st_ref.1, bf16[10,4,1024]{2,1,0:T(4,128)(2,1)} %bitcast.5, bf16[8,128]{1,0:T(8,128)(2,1)} %bitcast.8, s32[8,128]{1,0:T(8,128)} %bitcast.7, s32[4,1024]{1,0:T(4,128)} %src_ref.1, s32[4,64]{1,0:T(4,128)} %bitcast.9, bf16[10,4,625]{2,1,0:T(4,128)(2,1)} %bitcast.6), custom_call_target="tpu_custom_call" | custom-call | tf_op jit(solution)/shard_map/pallas_call | solution.py:542
  93.5 1.2 %copy.9 = f32[1,256]{1,0:T(1,128)} copy(f32[1,256]{1,0:T(1,128)} %shard_map.73) | data formatting | bytes 2048
